TPU v7x, 32 devices: a whole 2x2x4 slice. The times are simulated.
32 devices in a mesh: jobs: 2 (over x), seq: 16 (over z, y, core).
Axes of the slice: x: 2, y: 2, z: 4, core: 2. Of those that a mesh axis runs over, the one named last changes fastest.
Arguments:
- queries: bfloat16 [1024, 4096], P(('jobs', 'seq')), parts along dimension 0, may hold values from -12 to 12
- keys: bfloat16 [1024, 4096], P(('jobs', 'seq')), parts along dimension 0, may hold values from -6 to 6
- values: bfloat16 [1024, 4096], P(('jobs', 'seq')), parts along dimension 0, may hold values from -6 to 6
- live_counts: int32 [2, 16], P('jobs', 'seq'), parts along dimension 0, may hold values from 4 to 16, as said below
- merge_dest: int32 [2, 1024], P('jobs', 'seq'), parts along dimension 0, may hold values from 0 to 15, as said below
- latents: float32 [2, 1024, 64], P('jobs', 'seq'), parts along dimension 0, may hold values from -6 to 6
- guidance: float32 [2], P('jobs'), parts along dimension 0, may hold values from 3 to 6
- step_index: int32 [2], P('jobs'), parts along dimension 0, may hold values from 0 to 980
- out_weight: bfloat16 [4096, 64], replicated, may hold values from -0.09375 to 0.09375
Outputs:
- denoised: float32 [2, 1024, 64], P('jobs', 'seq'), parts along dimension 0
- merged_next: float32 [2, 256, 64], P('jobs', 'seq'), parts along dimension 0
There are 2 independent parts, one for each index of `jobs`. A program takes and returns all parts, laid end to end along the dimension named above; an argument that names none is the same for every part. Nothing has to cross between parts.
Inputs may be any that keep to these rules, and one draw needn't show every extreme that they name: `live_counts`: in every video some merge group has exactly 16 live slots. `merge_dest`: each token names a slot of its own merge group below that group's live count, and every live slot is named by at least one token.
All inputs are finite; a program needn't handle non-finite values.
Results may differ from a plain program's by a relative error of at most 0.0031.
Values may be sent and summed in bfloat16 or wider, within the bound.
No kernel may reach another device: no remote copies, remote signals or barrier semaphores. Data moves between devices by JAX's collectives and lax.ppermute only.
A program may use at most 64 MiB of HBM per device.

v0:
```python
import math
import jax
import jax.numpy as jnp
from jax import lax
from jax.sharding import PartitionSpec as P

HEADS = 32
HD = 128
TIMESTEPS = 1000
STRIDE = 20
neg_big = -1e30
shift_value = 5.0


def sigma_of(step_value):
    frac = 1.0 - step_value / TIMESTEPS
    return shift_value * frac / (1.0 + (shift_value - 1.0) * frac)


def attend_branch(query_rows, key_rows, value_rows, key_live, score_scale):
    total_rows = query_rows.shape[0]
    block_rows = 512 if total_rows % 512 == 0 else total_rows

    def one_block(query_block):
        scores = (
            lax.dot_general(
                query_block, key_rows, (((1,), (1,)), ((), ())), preferred_element_type=jnp.float32
            )
            * score_scale
        )
        scores = jnp.where(key_live[None, :], scores, neg_big)
        row_top = jnp.max(scores, axis=-1, keepdims=True)
        weights = jnp.exp(scores - row_top)
        probabilities = (weights / jnp.sum(weights, axis=-1, keepdims=True)).astype(jnp.bfloat16)
        return jnp.dot(probabilities, value_rows, preferred_element_type=jnp.float32).astype(
            jnp.bfloat16
        )

    blocks = query_rows.reshape(total_rows // block_rows, block_rows, query_rows.shape[1])
    return lax.map(one_block, blocks).reshape(total_rows, query_rows.shape[1])


def local(
    queries, keys, values, live_counts, merge_dest, latents, guidance, step_index, out_weight
):
    groups = lax.axis_size("seq")
    device = lax.axis_index("seq")
    pair_count = groups // 2
    local_rows, columns = queries.shape
    cap_half = local_rows // 2
    videos = guidance.shape[0]
    feature_width = columns // videos
    per_device = columns // groups
    item_count = per_device // HD
    branch_slots = groups * cap_half
    score_scale = 1.0 / math.sqrt(HD)
    counts_all = lax.all_gather(live_counts, "seq", axis=1, tiled=True)
    query_in, key_in, value_in = (
        lax.all_to_all(queries, "seq", split_axis=1, concat_axis=0, tiled=True),
        lax.all_to_all(keys, "seq", split_axis=1, concat_axis=0, tiled=True),
        lax.all_to_all(values, "seq", split_axis=1, concat_axis=0, tiled=True),
    )
    count_grid = counts_all.reshape(videos, 2, pair_count).transpose(0, 2, 1)
    live_slots = (
        jnp.arange(cap_half, dtype=jnp.int32)[None, None, None, :] < count_grid[..., None]
    ).reshape(videos, branch_slots)
    guided_parts = []
    head_numbers = []
    for item_index in range(item_count):
        global_item = device * item_count + item_index
        video_index = global_item // HEADS
        key_live = live_slots[video_index]
        col_start = item_index * HD
        branch_outs = []
        for branch_no in range(2):
            row_start = branch_no * branch_slots
            branch_outs.append(
                attend_branch(
                    query_in[row_start : row_start + branch_slots, col_start : col_start + HD],
                    key_in[row_start : row_start + branch_slots, col_start : col_start + HD],
                    value_in[row_start : row_start + branch_slots, col_start : col_start + HD],
                    key_live,
                    score_scale,
                )
            )
        conditioned = branch_outs[0].astype(jnp.float32)
        uncond = branch_outs[1].astype(jnp.float32)
        guided_parts.append(
            (uncond + guidance[video_index] * (conditioned - uncond)).astype(jnp.bfloat16)
        )
        head_numbers.append(global_item % HEADS)
    stacked = jnp.concatenate(guided_parts, axis=1)
    ordered = (
        stacked.reshape(pair_count, 2, cap_half, per_device)
        .transpose(1, 0, 2, 3)
        .reshape(groups * cap_half, per_device)
    )
    mixed = lax.all_to_all(ordered, "seq", split_axis=0, concat_axis=1, tiled=True)
    merged = jnp.einsum(
        "jva,ac->vjc",
        mixed.reshape(cap_half, videos, feature_width),
        out_weight,
        preferred_element_type=jnp.float32,
    )
    onehot = (merge_dest[..., None] == jnp.arange(cap_half, dtype=jnp.int32)).astype(jnp.float32)
    velocity = jnp.einsum("vrj,vjc->vrc", onehot, merged, precision=lax.Precision.HIGHEST)
    step_value = step_index.astype(jnp.float32)
    sigma_now = sigma_of(step_value)
    sigma_next = sigma_of(step_value + float(STRIDE))
    denoised = latents - sigma_now[:, None, None] * velocity
    advanced = latents + (sigma_next - sigma_now)[:, None, None] * velocity
    slot_sums = jnp.einsum("vrj,vrc->vjc", onehot, advanced, precision=lax.Precision.HIGHEST)
    slot_tally = jnp.sum(onehot, axis=1)
    merged_next = slot_sums / jnp.maximum(slot_tally, 1.0)[..., None]
    return (denoised, merged_next)


def solution(mesh):
    placed = (
        P(("jobs", "seq"), None),
        P(("jobs", "seq"), None),
        P(("jobs", "seq"), None),
        P("jobs", "seq"),
        P("jobs", "seq"),
        P("jobs", "seq", None),
        P("jobs"),
        P("jobs"),
        P(),
    )
    return jax.shard_map(
        local,
        mesh=mesh,
        in_specs=placed,
        out_specs=(P("jobs", "seq", None), P("jobs", "seq", None)),
        check_vma=False,
    )
```

profile of v0, /device:TPU:0, one launch (start us, length us, event | category | flops | bytes accessed | tf_op | source)
XLA Modules:
  0.0 69.5 jit_solution(11512666287636155792)
XLA Ops:
  0.6 0.0 copy-start
  0.6 1.7 %copy.78 = bf16[4,16,8,256]{3,2,0,1:T(8,128)(2,1)} copy(bf16[4,16,8,256]{3,2,1,0:T(8,128)(2,1)} %bitcast.66) | data formatting | bytes 524288 | tf_op jit(solution)/shard_map/all_to_all | solution.py:59
  2.4 0.0 copy-start.1
  2.4 7.5 %all-to-all-start = ((bf16[32,16,256]{2,0,1:T(8,128)(2,1)}), bf16[32,16,256]{2,0,1:T(8,128)(2,1)S(1)}, u32[]{:S(2)}, u32[]{:S(2)}) async-start(bf16[32,16,256]{2,0,1:T(8,128)(2,1)} %bitcast.62), calls=%async_computation | async-start | bytes 524288 | tf_op jit(solution)/shard_map/all_to_all | solution.py:59
  9.9 0.0 copy-done.1
  9.9 0.7 %copy.77 = bf16[4,16,8,256]{3,2,0,1:T(8,128)(2,1)} copy(bf16[4,16,8,256]{3,2,1,0:T(8,128)(2,1)S(1)} %bitcast.67) | data formatting | bytes 524288 | tf_op jit(solution)/shard_map/all_to_all | solution.py:60
  10.7 9.3 %all-to-all-done = bf16[32,16,256]{2,0,1:T(8,128)(2,1)S(1)} async-done(((bf16[32,16,256]{2,0,1:T(8,128)(2,1)}), bf16[32,16,256]{2,0,1:T(8,128)(2,1)S(1)}, u32[]{:S(2)}, u32[]{:S(2)}) %all-to-all-start) | async-done | bytes 262176 | tf_op jit(solution)/shard_map/all_to_all | solution.py:59
  19.9 0.0 copy-start.2
  19.9 3.7 %all-to-all-start.1 = ((bf16[32,16,256]{2,0,1:T(8,128)(2,1)}), bf16[32,16,256]{2,0,1:T(8,128)(2,1)S(1)}, u32[]{:S(2)}, u32[]{:S(2)}) async-start(bf16[32,16,256]{2,0,1:T(8,128)(2,1)} %bitcast.61), calls=%async_computation.1 | async-start | bytes 524288 | tf_op jit(solution)/shard_map/all_to_all | solution.py:60
  24.3 0.0 copy-start.5
  24.3 0.6 copy-done.5
  24.9 0.6 dynamic-slice.4
  25.5 0.7 bitcast_dynamic-update-slice_fusion
  26.2 12.4 %all-reduce = s32[16]{0:T(128)S(1)} all-reduce(s32[16]{0:T(128)S(1)} %bitcast_dynamic-update-slice_fusion), channel_id=1, replica_groups=mesh['jobs'=2,'seq'=16] {'seq'}, use_global_device_ids=true, to_apply=%add | all-reduce | flops 16 | bytes 128
  38.6 0.1 reshape.221
  38.7 0.1 copy.42
  38.7 0.1 iota_compare_fusion.4
  38.8 0.1 lt.36
  38.9 0.0 copy-done.2
  38.9 0.7 %copy.76 = bf16[4,16,8,256]{3,2,0,1:T(8,128)(2,1)} copy(bf16[4,16,8,256]{3,2,1,0:T(8,128)(2,1)S(1)} %bitcast.68) | data formatting | bytes 524288 | tf_op jit(solution)/shard_map/all_to_all | solution.py:61
  40.3 0.0 all-to-all-done.1
  40.3 3.5 %all-to-all-start.2 = ((bf16[32,16,256]{2,0,1:T(8,128)(2,1)}), bf16[32,16,256]{2,0,1:T(8,128)(2,1)S(1)}, u32[]{:S(2)}, u32[]{:S(2)}) async-start(bf16[32,16,256]{2,0,1:T(8,128)(2,1)} %bitcast.60), calls=%async_computation.2 | async-start | bytes 524288 | tf_op jit(solution)/shard_map/all_to_all | solution.py:61
  43.9 0.2 fusion.35
  44.1 0.2 fusion.36
  44.3 0.1 fusion.8
  44.4 0.2 fusion.37
  44.6 0.2 fusion.38
  44.8 9.0 %all-to-all-done.2 = bf16[32,16,256]{2,0,1:T(8,128)(2,1)S(1)} async-done(((bf16[32,16,256]{2,0,1:T(8,128)(2,1)}), bf16[32,16,256]{2,0,1:T(8,128)(2,1)S(1)}, u32[]{:S(2)}, u32[]{:S(2)}) %all-to-all-start.2) | async-done | bytes 262176 | tf_op jit(solution)/shard_map/all_to_all | solution.py:61
  53.8 0.2 convolution_convert_fusion
  54.1 0.1 fusion.7
  54.2 0.2 convolution_convert_fusion.1
  54.4 0.1 fusion.6
  54.5 0.2 convolution_convert_fusion.2
  54.7 0.1 fusion.5
  54.8 0.2 convolution_convert_fusion.3
  55.1 0.1 fusion.11
  55.1 0.7 pad_maximum_fusion
  55.8 3.5 %all-to-all-start.3 = ((bf16[16,16,256]{2,1,0:T(8,128)(2,1)}), bf16[16,16,256]{2,1,0:T(8,128)(2,1)S(1)}, u32[]{:S(2)}, u32[]{:S(2)}) async-start(bf16[16,16,256]{2,1,0:T(8,128)(2,1)} %bitcast.23), calls=%async_computation.3 | async-start | bytes 262144 | tf_op jit(solution)/shard_map/all_to_all | solution.py:98
  59.3 0.0 copy-start.4
  59.3 0.6 copy-done.4
  59.9 0.1 convert_reduce_fusion
  60.8 6.3 %all-to-all-done.3 = bf16[16,16,256]{2,1,0:T(8,128)(2,1)S(1)} async-done(((bf16[16,16,256]{2,1,0:T(8,128)(2,1)}), bf16[16,16,256]{2,1,0:T(8,128)(2,1)S(1)}, u32[]{:S(2)}, u32[]{:S(2)}) %all-to-all-start.3) | async-done | bytes 131104 | tf_op jit(solution)/shard_map/all_to_all | solution.py:98
  67.2 0.0 copy-done
  67.2 0.0 copy-start.3
  67.2 0.2 fusion.39
  67.4 0.5 copy-done.3
  67.9 0.8 %bitcast_subtract_fusion = (f32[1,64,64]{2,1,0:T(8,128)}, f32[64,64]{1,0:T(8,128)S(1)}) fusion(f32[1,64,64]{2,1,0:T(8,128)S(1)} %copy-done.3, f32[]{:T(128)} %bitcast, f32[16,64]{1,0:T(8,128)S(1)} %fusion.39, s32[64]{0:T(128)S(1)} %bitcast.86), kind=kOutput, calls=%fused_computation.52 | convolution fusion | flops 795648 | bytes 53508 | tf_op jit(solution)/shard_map/vrj,vjc->vrc/dot_general | solution.py:106
  68.8 0.7 %fusion.4 = f32[1,16,64]{2,1,0:T(8,128)} fusion(f32[1,64,64]{2,1,0:T(8,128)S(1)} %copy-done.3, f32[64,64]{1,0:T(8,128)S(1)} %get-tuple-element.65, f32[]{:T(128)} %bitcast.27, f32[16]{0:T(128)S(1)} %broadcast_maximum_fusion, s32[64]{0:T(128)S(1)} %bitcast.87), kind=kOutput, calls=%fused_computation.13 | convolution fusion | flops 796672 | bytes 37188 | tf_op jit(solution)/shard_map/vrj,vrc->vjc/dot_general | solution.py:112
  (3 shorter events, 0.0 us)
Async XLA Ops:
  0.6 66.5 %copy-start = (bf16[4096,64]{0,1:T(8,128)(2,1)S(1)}, bf16[4096,64]{0,1:T(8,128)(2,1)}, u32[]{:S(2)}) copy-start(bf16[4096,64]{0,1:T(8,128)(2,1)} %param.17) | copy-start | bytes 1572868
  2.4 7.6 %copy-start.1 = (bf16[32,4096]{1,0:T(8,128)(2,1)S(1)}, bf16[32,4096]{1,0:T(8,128)(2,1)}, u32[]{:S(2)}) copy-start(bf16[32,4096]{1,0:T(8,128)(2,1)} %param.10) | copy-start | bytes 786436
  2.4 17.6 %all-to-all-start = ((bf16[32,16,256]{2,0,1:T(8,128)(2,1)}), bf16[32,16,256]{2,0,1:T(8,128)(2,1)S(1)}, u32[]{:S(2)}, u32[]{:S(2)}) async-start(bf16[32,16,256]{2,0,1:T(8,128)(2,1)} %bitcast.62), calls=%async_computation | async-start | bytes 524288 | tf_op jit(solution)/shard_map/all_to_all | solution.py:59
  19.9 19.0 %copy-start.2 = (bf16[32,4096]{1,0:T(8,128)(2,1)S(1)}, bf16[32,4096]{1,0:T(8,128)(2,1)}, u32[]{:S(2)}) copy-start(bf16[32,4096]{1,0:T(8,128)(2,1)} %param.11) | copy-start | bytes 786436
  19.9 20.4 %all-to-all-start.1 = ((bf16[32,16,256]{2,0,1:T(8,128)(2,1)}), bf16[32,16,256]{2,0,1:T(8,128)(2,1)S(1)}, u32[]{:S(2)}, u32[]{:S(2)}) async-start(bf16[32,16,256]{2,0,1:T(8,128)(2,1)} %bitcast.61), calls=%async_computation.1 | async-start | bytes 524288 | tf_op jit(solution)/shard_map/all_to_all | solution.py:60
  24.3 0.7 copy-start.5
  40.3 13.5 %all-to-all-start.2 = ((bf16[32,16,256]{2,0,1:T(8,128)(2,1)}), bf16[32,16,256]{2,0,1:T(8,128)(2,1)S(1)}, u32[]{:S(2)}, u32[]{:S(2)}) async-start(bf16[32,16,256]{2,0,1:T(8,128)(2,1)} %bitcast.60), calls=%async_computation.2 | async-start | bytes 524288 | tf_op jit(solution)/shard_map/all_to_all | solution.py:61
  55.8 11.4 %all-to-all-start.3 = ((bf16[16,16,256]{2,1,0:T(8,128)(2,1)}), bf16[16,16,256]{2,1,0:T(8,128)(2,1)S(1)}, u32[]{:S(2)}, u32[]{:S(2)}) async-start(bf16[16,16,256]{2,1,0:T(8,128)(2,1)} %bitcast.23), calls=%async_computation.3 | async-start | bytes 262144 | tf_op jit(solution)/shard_map/all_to_all | solution.py:98
  59.3 0.7 copy-start.4
  67.2 0.8 %copy-start.3 = (f32[1,64,64]{2,1,0:T(8,128)S(1)}, f32[1,64,64]{2,1,0:T(8,128)}, u32[]{:S(2)}) copy-start(f32[1,64,64]{2,1,0:T(8,128)} %param.14) | copy-start | bytes 49156
where the time goes:
time: 70.2 us; the launch traced here: 69.5 us
  waiting for transfers between devices  24.6 us (35%)
  starting transfers between devices  18.3 us (26%)
  blocking collectives  12.4 us (18%)
  local copies, waits for them, and re-layouts  6.53 us (9%)
  matrix products  3.66 us (5%)
  between operations  2.84 us (4%)
  other arithmetic  1.2 us (2%)
    unnamed x1, blocking collectives  12.4 us
    all_to_all x1, waiting for transfers between devices, local(): lax.all_to_all(queries, 'seq', split_axis=1, concat_axis=0, tiled=True)  9.28 us
    all_to_all x1, waiting for transfers between devices, local(): lax.all_to_all(values, 'seq', split_axis=1, concat_axis=0, tiled=True)  9.02 us
    all_to_all x1, starting transfers between devices, local(): lax.all_to_all(queries, 'seq', split_axis=1, concat_axis=0, tiled=True)  7.55 us
    all_to_all x1, waiting for transfers between devices, local(): lax.all_to_all(ordered, 'seq', split_axis=0, concat_axis=1, tiled=True)  6.34 us
    all_to_all x1, starting transfers between devices, local(): lax.all_to_all(keys, 'seq', split_axis=1, concat_axis=0, tiled=True)  3.66 us
    all_to_all x1, starting transfers between devices, local(): lax.all_to_all(values, 'seq', split_axis=1, concat_axis=0, tiled=True)  3.54 us
    all_to_all x1, starting transfers between devices, local(): lax.all_to_all(ordered, 'seq', split_axis=0, concat_axis=1, tiled=True)  3.51 us
  transfers between devices with their start and end apart: 4, of which 3 were waited for; matrix products, arithmetic and copies ran while one was open for 6% of the time, Pallas kernels for 0%

commit v1 on v0

--- a/solution.py
+++ b/solution.py
@@ -95,7 +95,11 @@
         .transpose(1, 0, 2, 3)
         .reshape(groups * cap_half, per_device)
     )
-    mixed = lax.all_to_all(ordered, "seq", split_axis=0, concat_axis=1, tiled=True)
+    after = lax.axis_size("seq")
+    val = jnp.split(ordered, after, 0)
+    z_new = jnp.stack(val, 0)
+    tile_out = lax.all_to_all(z_new, "seq", 0, 0)
+    mixed = jnp.concatenate(tile_out, 1)
     merged = jnp.einsum(
         "jva,ac->vjc",
         mixed.reshape(cap_half, videos, feature_width),

time: 70.2 us -> 79.1 us (1.13)
  local copies, waits for them, and re-layouts: 6.53 us -> 16 us
    unnamed x15 -> x30, local copies, waits for them, and re-layouts: 3.08 us -> 12 us
  transfers between devices with their start and end apart: 4 -> 4, of which waited for: 3 -> 3; matrix products, arithmetic and copies ran while one was open for 6% -> 5% of each run, Pallas kernels for 0% -> 0%
where the time goes in v1:
time: 79.1 us; the launch traced here: 78.4 us
  waiting for transfers between devices  24.6 us (31%)
  starting transfers between devices  18.3 us (23%)
  local copies, waits for them, and re-layouts  16 us (20%)
  blocking collectives  12.4 us (16%)
  matrix products  3.66 us (5%)
  between operations  2.85 us (4%)
    unnamed x1, blocking collectives  12.4 us
    unnamed x30, local copies, waits for them, and re-layouts  12 us
    all_to_all x1, waiting for transfers between devices, local(): lax.all_to_all(queries, 'seq', split_axis=1, concat_axis=0, tiled=True)  9.28 us
    all_to_all x1, waiting for transfers between devices, local(): lax.all_to_all(values, 'seq', split_axis=1, concat_axis=0, tiled=True)  9.02 us
    all_to_all x1, starting transfers between devices, local(): lax.all_to_all(queries, 'seq', split_axis=1, concat_axis=0, tiled=True)  7.55 us
    all_to_all x1, waiting for transfers between devices, local(): tile_out = lax.all_to_all(z_new, 'seq', 0, 0)  6.34 us
    all_to_all x1, starting transfers between devices, local(): lax.all_to_all(keys, 'seq', split_axis=1, concat_axis=0, tiled=True)  3.66 us
    all_to_all x1, starting transfers between devices, local(): lax.all_to_all(values, 'seq', split_axis=1, concat_axis=0, tiled=True)  3.54 us
  transfers between devices with their start and end apart: 4, of which 3 were waited for; matrix products, arithmetic and copies ran while one was open for 5% of the time, Pallas kernels for 0%

profile of v1, /device:TPU:0, one launch (start us, length us, event | category | flops | bytes accessed | tf_op | source)
XLA Modules:
  0.0 78.4 jit_solution(7851215365985310574)
XLA Ops:
  0.6 0.0 copy-start
  0.6 1.7 %copy.78 = bf16[4,16,8,256]{3,2,0,1:T(8,128)(2,1)} copy(bf16[4,16,8,256]{3,2,1,0:T(8,128)(2,1)} %bitcast.146) | data formatting | bytes 524288 | tf_op jit(solution)/shard_map/all_to_all | solution.py:59
  2.4 0.0 copy-start.1
  2.4 7.5 %all-to-all-start = ((bf16[32,16,256]{2,0,1:T(8,128)(2,1)}), bf16[32,16,256]{2,0,1:T(8,128)(2,1)S(1)}, u32[]{:S(2)}, u32[]{:S(2)}) async-start(bf16[32,16,256]{2,0,1:T(8,128)(2,1)} %bitcast.126), calls=%async_computation | async-start | bytes 524288 | tf_op jit(solution)/shard_map/all_to_all | solution.py:59
  9.9 0.0 copy-done.1
  9.9 0.7 copy.77
  10.7 9.3 %all-to-all-done = bf16[32,16,256]{2,0,1:T(8,128)(2,1)S(1)} async-done(((bf16[32,16,256]{2,0,1:T(8,128)(2,1)}), bf16[32,16,256]{2,0,1:T(8,128)(2,1)S(1)}, u32[]{:S(2)}, u32[]{:S(2)}) %all-to-all-start) | async-done | bytes 262176 | tf_op jit(solution)/shard_map/all_to_all | solution.py:59
  19.9 0.0 copy-start.2
  19.9 3.7 %all-to-all-start.1 = ((bf16[32,16,256]{2,0,1:T(8,128)(2,1)}), bf16[32,16,256]{2,0,1:T(8,128)(2,1)S(1)}, u32[]{:S(2)}, u32[]{:S(2)}) async-start(bf16[32,16,256]{2,0,1:T(8,128)(2,1)} %bitcast.125), calls=%async_computation.1 | async-start | bytes 524288 | tf_op jit(solution)/shard_map/all_to_all | solution.py:60
  24.3 0.0 copy-start.5
  24.3 0.6 copy-done.5
  24.9 0.6 dynamic-slice.4
  25.5 0.7 bitcast_dynamic-update-slice_fusion
  26.2 12.4 %all-reduce = s32[16]{0:T(128)S(1)} all-reduce(s32[16]{0:T(128)S(1)} %bitcast_dynamic-update-slice_fusion), channel_id=1, replica_groups=mesh['jobs'=2,'seq'=16] {'seq'}, use_global_device_ids=true, to_apply=%add | all-reduce | flops 16 | bytes 128
  38.6 0.1 reshape.220
  38.7 0.1 copy.42
  38.7 0.1 iota_compare_fusion.4
  38.8 0.1 lt.36
  38.9 0.0 copy-done.2
  38.9 0.7 copy.76
  40.3 0.0 all-to-all-done.1
  40.3 3.5 %all-to-all-start.2 = ((bf16[32,16,256]{2,0,1:T(8,128)(2,1)}), bf16[32,16,256]{2,0,1:T(8,128)(2,1)S(1)}, u32[]{:S(2)}, u32[]{:S(2)}) async-start(bf16[32,16,256]{2,0,1:T(8,128)(2,1)} %bitcast.124), calls=%async_computation.2 | async-start | bytes 524288 | tf_op jit(solution)/shard_map/all_to_all | solution.py:61
  43.9 0.2 fusion.35
  44.1 0.2 fusion.36
  44.3 0.1 fusion.8
  44.4 0.2 fusion.37
  44.6 0.2 fusion.38
  44.8 9.0 %all-to-all-done.2 = bf16[32,16,256]{2,0,1:T(8,128)(2,1)S(1)} async-done(((bf16[32,16,256]{2,0,1:T(8,128)(2,1)}), bf16[32,16,256]{2,0,1:T(8,128)(2,1)S(1)}, u32[]{:S(2)}, u32[]{:S(2)}) %all-to-all-start.2) | async-done | bytes 262176 | tf_op jit(solution)/shard_map/all_to_all | solution.py:61
  53.8 0.2 convolution_convert_fusion
  54.1 0.1 fusion.7
  54.2 0.2 convolution_convert_fusion.1
  54.4 0.1 fusion.6
  54.5 0.2 convolution_convert_fusion.2
  54.7 0.1 fusion.5
  54.8 0.2 convolution_convert_fusion.3
  55.1 0.1 fusion.11
  55.1 0.6 constant_dynamic-update-slice_fusion.15
  55.7 0.6 constant_dynamic-update-slice_fusion.14
  56.3 0.6 constant_dynamic-update-slice_fusion.13
  56.9 0.6 constant_dynamic-update-slice_fusion.12
  57.5 0.6 constant_dynamic-update-slice_fusion.11
  58.1 0.6 constant_dynamic-update-slice_fusion.10
  58.7 0.6 constant_dynamic-update-slice_fusion.9
  59.3 0.6 constant_dynamic-update-slice_fusion.8
  59.9 0.6 constant_dynamic-update-slice_fusion.7
  60.5 0.6 constant_dynamic-update-slice_fusion.6
  61.1 0.6 constant_dynamic-update-slice_fusion.5
  61.7 0.6 constant_dynamic-update-slice_fusion.4
  62.3 0.6 constant_dynamic-update-slice_fusion.3
  62.9 0.6 constant_dynamic-update-slice_fusion.2
  63.5 0.6 constant_dynamic-update-slice_fusion.1
  64.1 0.6 constant_dynamic-update-slice_fusion
  64.7 3.5 %all-to-all-start.3 = ((bf16[16,16,256]{2,1,0:T(8,128)(2,1)}), bf16[16,16,256]{2,1,0:T(8,128)(2,1)S(1)}, u32[]{:S(2)}, u32[]{:S(2)}) async-start(bf16[16,16,256]{2,1,0:T(8,128)(2,1)} %constant_dynamic-update-slice_fusion), calls=%async_computation.3 | async-start | bytes 262144 | tf_op jit(solution)/shard_map/all_to_all | solution.py:101
  68.2 0.0 copy-start.4
  68.2 0.6 copy-done.4
  68.8 0.1 convert_reduce_fusion
  69.7 6.3 %all-to-all-done.3 = bf16[16,16,256]{2,1,0:T(8,128)(2,1)S(1)} async-done(((bf16[16,16,256]{2,1,0:T(8,128)(2,1)}), bf16[16,16,256]{2,1,0:T(8,128)(2,1)S(1)}, u32[]{:S(2)}, u32[]{:S(2)}) %all-to-all-start.3) | async-done | bytes 131104 | tf_op jit(solution)/shard_map/all_to_all | solution.py:101
  76.1 0.0 copy-done
  76.1 0.0 copy-start.3
  76.1 0.2 fusion.39
  76.3 0.5 copy-done.3
  76.8 0.8 %bitcast_subtract_fusion = (f32[1,64,64]{2,1,0:T(8,128)}, f32[64,64]{1,0:T(8,128)S(1)}) fusion(f32[1,64,64]{2,1,0:T(8,128)S(1)} %copy-done.3, f32[]{:T(128)} %bitcast, f32[16,64]{1,0:T(8,128)S(1)} %fusion.39, s32[64]{0:T(128)S(1)} %bitcast.166), kind=kOutput, calls=%fused_computation.68 | convolution fusion | flops 795648 | bytes 53508 | tf_op jit(solution)/shard_map/vrj,vjc->vrc/dot_general | solution.py:110
  77.7 0.7 fusion.4
  (4 shorter events, 0.0 us)
Async XLA Ops:
  0.6 75.4 %copy-start = (bf16[4096,64]{0,1:T(8,128)(2,1)S(1)}, bf16[4096,64]{0,1:T(8,128)(2,1)}, u32[]{:S(2)}) copy-start(bf16[4096,64]{0,1:T(8,128)(2,1)} %param.17) | copy-start | bytes 1572868
  2.4 7.6 %copy-start.1 = (bf16[32,4096]{1,0:T(8,128)(2,1)S(1)}, bf16[32,4096]{1,0:T(8,128)(2,1)}, u32[]{:S(2)}) copy-start(bf16[32,4096]{1,0:T(8,128)(2,1)} %param.10) | copy-start | bytes 786436
  2.4 17.6 %all-to-all-start = ((bf16[32,16,256]{2,0,1:T(8,128)(2,1)}), bf16[32,16,256]{2,0,1:T(8,128)(2,1)S(1)}, u32[]{:S(2)}, u32[]{:S(2)}) async-start(bf16[32,16,256]{2,0,1:T(8,128)(2,1)} %bitcast.126), calls=%async_computation | async-start | bytes 524288 | tf_op jit(solution)/shard_map/all_to_all | solution.py:59
  19.9 19.0 %copy-start.2 = (bf16[32,4096]{1,0:T(8,128)(2,1)S(1)}, bf16[32,4096]{1,0:T(8,128)(2,1)}, u32[]{:S(2)}) copy-start(bf16[32,4096]{1,0:T(8,128)(2,1)} %param.11) | copy-start | bytes 786436
  19.9 20.4 %all-to-all-start.1 = ((bf16[32,16,256]{2,0,1:T(8,128)(2,1)}), bf16[32,16,256]{2,0,1:T(8,128)(2,1)S(1)}, u32[]{:S(2)}, u32[]{:S(2)}) async-start(bf16[32,16,256]{2,0,1:T(8,128)(2,1)} %bitcast.125), calls=%async_computation.1 | async-start | bytes 524288 | tf_op jit(solution)/shard_map/all_to_all | solution.py:60
  24.3 0.7 copy-start.5
  40.3 13.5 %all-to-all-start.2 = ((bf16[32,16,256]{2,0,1:T(8,128)(2,1)}), bf16[32,16,256]{2,0,1:T(8,128)(2,1)S(1)}, u32[]{:S(2)}, u32[]{:S(2)}) async-start(bf16[32,16,256]{2,0,1:T(8,128)(2,1)} %bitcast.124), calls=%async_computation.2 | async-start | bytes 524288 | tf_op jit(solution)/shard_map/all_to_all | solution.py:61
  64.7 11.4 %all-to-all-start.3 = ((bf16[16,16,256]{2,1,0:T(8,128)(2,1)}), bf16[16,16,256]{2,1,0:T(8,128)(2,1)S(1)}, u32[]{:S(2)}, u32[]{:S(2)}) async-start(bf16[16,16,256]{2,1,0:T(8,128)(2,1)} %constant_dynamic-update-slice_fusion), calls=%async_computation.3 | async-start | bytes 262144 | tf_op jit(solution)/shard_map/all_to_all | solution.py:101
  68.2 0.7 copy-start.4
  76.1 0.8 copy-start.3
